TPU v7x, 128 devices: a whole 4x4x4 slice. The times are simulated.
128 devices in a mesh: dom: 128 (over x, z, y, core).
Axes of the slice: x: 4, y: 4, z: 4, core: 2. Of those that a mesh axis runs over, the one named last changes fastest.
Arguments:
- adjoint_end: bfloat16 [1024, 384, 256], P('dom'), may hold values from -6 to 6
- operator_blocks: bfloat16 [1024, 6, 384, 384], P('dom'), may hold values from -0.125 to 0.125
- block_cols: int32 [1024, 6], P('dom'), may hold values from -1 to 15, as said below
- halo_send: int32 [128, 4, 2], P('dom'), may hold values from -1 to 7, as said below
- wet_cells: int32 [1024, 128], P('dom'), may hold values 0 or 1
- gauge_cells: int32 [256], replicated, may hold values from 0 to 131071
- window_first: int32 [256], replicated, may hold values from 0 to 1
- window_len: int32 [256], replicated, may hold values from 1 to 2
- gauge_gain: float32 [256], replicated, may hold values from 0.5 to 4
- snapshots: float32 [2, 1024, 384], P(None, 'dom'), may hold values from -27 to 27, as said below
Outputs:
- adjoint_start: bfloat16 [1024, 384, 256], P('dom')
- sensitivity: float32 [1024, 128, 256], P('dom')
Inputs may be any that keep to these rules, and one draw needn't show every extreme that they name: `block_cols`: in each row entry 0 is the row's own local block; live entries come first and -1 fills the rest; received slots named are only those whose sending device exists. `halo_send`: for each device and neighbour o the 2 blocks are distinct; -1 exactly where device d + off_o does not exist. `snapshots`: nonzero values.
All inputs are finite; a program needn't handle non-finite values. No bound on the sum of `wet_cells` on one device may be relied on, other than what follows from the above.
Results may differ from a plain program's by a relative error of at most 0.0013.
The roundings to bfloat16 on the way count: a program that leaves them out, or rounds other values in their place, can miss the bound.
Values may be sent and summed in bfloat16 or wider, within the bound.
A program may use at most 128 MiB of HBM per device.

v0:
```python
import jax
import jax.numpy as jnp
from jax import lax
from jax.sharding import PartitionSpec as P

neighbour_offsets = (-2, -1, 1, 2)


def passed_along(value, axis, by):
    devices = lax.axis_size(axis)
    pairs = [(i, i + by) for i in range(devices) if 0 <= i + by < devices]
    return lax.ppermute(value, axis, pairs)


def extended_state(adjoint, send_lists):
    owned = adjoint.shape[0]
    received = [None, None, None, None]
    for group, offset in enumerate(neighbour_offsets):
        received[group] = passed_along(
            adjoint[jnp.clip(send_lists[group], 0, owned - 1)], "dom", offset
        )
    return jnp.concatenate([adjoint] + received, axis=0)


def coupled_rows(extended, operator_blocks, block_cols):
    last = extended.shape[0] - 1
    picked = extended[jnp.clip(block_cols, 0, last)]
    picked = jnp.where((block_cols >= 0)[:, :, None, None], picked, jnp.zeros((), jnp.bfloat16))
    return jnp.einsum("bkij,bkjf->bif", operator_blocks, picked, preferred_element_type=jnp.float32)


def per_device(
    adjoint_end,
    operator_blocks,
    block_cols,
    halo_send,
    wet_cells,
    gauge_cells,
    window_first,
    window_len,
    gauge_gain,
    snapshots,
):
    owned = adjoint_end.shape[0]
    width = adjoint_end.shape[2]
    cell_count = wet_cells.shape[1]
    devices = lax.axis_size("dom")
    position = lax.axis_index("dom")
    send_lists = halo_send[0]
    cell_ids = position * (owned * cell_count) + jnp.arange(
        owned * cell_count, dtype=jnp.int32
    ).reshape(owned, cell_count)
    gauge_hit = (cell_ids[:, :, None] == gauge_cells[None, None, :]).astype(jnp.float32)
    wet_rows = jnp.tile(wet_cells.astype(jnp.float32), (1, 3))[:, :, None]
    padding = jnp.zeros((owned, 2 * cell_count, width), jnp.float32)
    adjoint = adjoint_end
    raw = jnp.zeros((owned, cell_count, width), jnp.float32)
    for step_index in range(snapshots.shape[0]):
        extended = extended_state(adjoint, send_lists)
        coupled = coupled_rows(extended, operator_blocks, block_cols)
        active = ((window_first <= step_index) & (step_index < window_first + window_len)).astype(
            jnp.float32
        ) * gauge_gain
        source_full = jnp.concatenate([gauge_hit * active[None, None, :], padding], axis=1)
        updated = wet_rows * (adjoint.astype(jnp.float32) + coupled) + source_full
        adjoint = updated.astype(jnp.bfloat16)
        saved = snapshots[step_index].reshape(owned, 3, cell_count)[:, :, :, None]
        raw = raw + jnp.sum(
            saved * adjoint.astype(jnp.float32).reshape(owned, 3, cell_count, width), axis=1
        )
    totals = lax.psum(jnp.sum(raw * raw, axis=(0, 1)), "dom")
    meansq = totals / (devices * owned * cell_count)
    sensitivity = raw * lax.rsqrt(meansq + 1e-06)[None, None, :]
    return (adjoint, sensitivity)


def solution(mesh):
    return jax.shard_map(
        per_device,
        mesh=mesh,
        in_specs=(
            P("dom", None, None),
            P("dom", None, None, None),
            P("dom", None),
            P("dom", None, None),
            P("dom", None),
            P(),
            P(),
            P(),
            P(),
            P(None, "dom", None),
        ),
        out_specs=(P("dom", None, None), P("dom", None, None)),
        check_vma=False,
    )
```

profile of v0, /device:TPU:0, one launch (start us, length us, event | category | flops | bytes accessed | tf_op | source)
XLA Modules:
  0.0 212.4 jit_solution(13992311859713529459)
XLA Ops:
  0.7 1.0 clamp_reduce_fusion
  1.8 2.7 %gather_fusion = bf16[2,384,256]{2,1,0:T(8,128)(2,1)} fusion(bf16[8,384,256]{2,1,0:T(8,128)(2,1)} %param.10, s32[1024]{0:T(1024)S(1)} %pad_clamp_fusion.4), kind=kCustom, calls=%fused_computation | custom fusion | bytes 786440 | tf_op jit(solution)/shard_map/gather | solution.py:20
  4.5 1.3 collective-permute-start
  5.8 2.7 %gather_fusion.1 = bf16[2,384,256]{2,1,0:T(8,128)(2,1)} fusion(bf16[8,384,256]{2,1,0:T(8,128)(2,1)} %param.10, s32[1024]{0:T(1024)S(1)} %pad_clamp_fusion.3), kind=kCustom, calls=%fused_computation.1 | custom fusion | bytes 786440 | tf_op jit(solution)/shard_map/gather | solution.py:20
  8.5 1.3 collective-permute-start.1
  9.9 2.7 %gather_fusion.2 = bf16[2,384,256]{2,1,0:T(8,128)(2,1)} fusion(bf16[8,384,256]{2,1,0:T(8,128)(2,1)} %param.10, s32[1024]{0:T(1024)S(1)} %pad_clamp_fusion.2), kind=kCustom, calls=%fused_computation.2 | custom fusion | bytes 786440 | tf_op jit(solution)/shard_map/gather | solution.py:20
  12.6 3.8 %collective-permute-start.2 = (bf16[2,384,256]{2,1,0:T(8,128)(2,1)}, bf16[2,384,256]{2,1,0:T(8,128)(2,1)}, u32[]{:S(2)}, u32[]{:S(2)}) collective-permute-start(bf16[2,384,256]{2,1,0:T(8,128)(2,1)} %gather_fusion.2), channel_id=1, source_target_pairs={{0,1},{1,2},{2,3},{3,4},{4,5},{5,6},{6,7},{7,8},{8,9},{9,10},{10,1... | collective-permute-start | bytes 1179656 | tf_op jit(solution)/shard_map/ppermute | solution.py:12
  16.4 2.7 %gather_fusion.3 = bf16[2,384,256]{2,1,0:T(8,128)(2,1)} fusion(bf16[8,384,256]{2,1,0:T(8,128)(2,1)} %param.10, s32[1024]{0:T(1024)S(1)} %pad_clamp_fusion.1), kind=kCustom, calls=%fused_computation.3 | custom fusion | bytes 786440 | tf_op jit(solution)/shard_map/gather | solution.py:20
  19.1 4.6 %collective-permute-start.3 = (bf16[2,384,256]{2,1,0:T(8,128)(2,1)}, bf16[2,384,256]{2,1,0:T(8,128)(2,1)}, u32[]{:S(2)}, u32[]{:S(2)}) collective-permute-start(bf16[2,384,256]{2,1,0:T(8,128)(2,1)} %gather_fusion.3), channel_id=1, source_target_pairs={{0,2},{1,3},{2,4},{3,5},{4,6},{5,7},{6,8},{7,9},{8,10},{9,11},{10,... | collective-permute-start | bytes 1179656 | tf_op jit(solution)/shard_map/ppermute | solution.py:12
  23.8 1.6 compare_select_fusion.1
  25.4 0.6 broadcast_compare_fusion
  26.0 0.1 constant_dynamic-update-slice_fusion.4
  26.1 0.6 reshape.180
  26.7 0.7 pad_clamp_fusion
  27.4 2.6 %copy.17 = bf16[8,384,256]{1,2,0:T(8,128)(2,1)} copy(bf16[8,384,256]{2,1,0:T(8,128)(2,1)} %param.10) | data formatting | bytes 3145728 | tf_op args[0]
  30.0 1.0 constant_dynamic-update-slice_fusion.2
  31.0 1.0 constant_dynamic-update-slice_fusion.1
  32.1 0.3 collective-permute-done.3
  32.4 1.0 constant_dynamic-update-slice_fusion
  33.4 6.3 %gather_fusion.4 = bf16[48,384,256]{2,1,0:T(8,128)(2,1)} fusion(bf16[16,384,256]{2,1,0:T(8,128)(2,1)S(1)} %constant_dynamic-update-slice_fusion, s32[1024]{0:T(1024)S(1)} %pad_clamp_fusion), kind=kCustom, calls=%fused_computation.4 | custom fusion | bytes 18874560 | tf_op jit(solution)/shard_map/gather | solution.py:27
  39.7 12.6 %copy.18 = bf16[8,6,384,256]{2,3,1,0:T(8,128)(2,1)} copy(bf16[8,6,384,256]{3,2,1,0:T(8,128)(2,1)} %bitcast.50) | data formatting | bytes 18874368 | tf_op jit(solution)/shard_map/gather | solution.py:27
  52.4 12.2 %constant_dynamic-update-slice_fusion.9 = (bf16[16,384,256]{1,2,0:T(8,128)(2,1)S(1)}, bf16[8,384,256]{1,2,0:T(8,128)(2,1)}) fusion(f32[8,128,256]{1,2,0:T(8,128)} %get-tuple-element.14, bf16[8,6,384,384]{3,2,1,0:T(8,128)(2,1)} %param.11, bf16[8,6,384,256]{2,3,1,0:T(8,128)(2,1)} %copy.18, pred[8,6]{1,0:T(8,128)(4,1)S(1)} %copy-done.15, ...), kind=kOutput, calls=%fused_computation.41 | convolution fusion | flops 3632529408 | bytes 29372464 | tf_op jit(solution)/shard_map/bkij,bkjf->bif/dot_general | solution.py:29
  64.6 2.9 %gather_fusion.5 = bf16[2,384,256]{1,2,0:T(8,128)(2,1)} fusion(bf16[8,384,256]{1,2,0:T(8,128)(2,1)} %get-tuple-element.19, s32[1024]{0:T(1024)} %copy-done.6), kind=kCustom, calls=%fused_computation.5 | custom fusion | bytes 786440 | tf_op jit(solution)/shard_map/gather | solution.py:20
  67.4 2.9 %gather_fusion.6 = bf16[2,384,256]{1,2,0:T(8,128)(2,1)} fusion(bf16[8,384,256]{1,2,0:T(8,128)(2,1)} %get-tuple-element.19, s32[1024]{0:T(1024)} %copy-done.8), kind=kCustom, calls=%fused_computation.6 | custom fusion | bytes 786440 | tf_op jit(solution)/shard_map/gather | solution.py:20
  70.3 1.3 collective-permute-start.4
  71.6 1.3 collective-permute-start.5
  72.9 0.7 slice_bitcast_fusion
  73.6 0.6 copy.19
  74.2 2.9 %gather_fusion.7 = bf16[2,384,256]{1,2,0:T(8,128)(2,1)} fusion(bf16[8,384,256]{1,2,0:T(8,128)(2,1)} %get-tuple-element.19, s32[1024]{0:T(1024)} %copy-done.7), kind=kCustom, calls=%fused_computation.7 | custom fusion | bytes 786440 | tf_op jit(solution)/shard_map/gather | solution.py:20
  77.1 2.9 %gather_fusion.8 = bf16[2,384,256]{1,2,0:T(8,128)(2,1)} fusion(bf16[8,384,256]{1,2,0:T(8,128)(2,1)} %get-tuple-element.19, s32[1024]{0:T(1024)} %copy-done.9), kind=kCustom, calls=%fused_computation.8 | custom fusion | bytes 786440 | tf_op jit(solution)/shard_map/gather | solution.py:20
  80.0 3.0 %copy.20 = f32[8,384,256]{2,1,0:T(8,128)} copy(bf16[8,384,256]{1,2,0:T(8,128)(2,1)} %get-tuple-element.19) | data formatting | bytes 4718592 | tf_op jit(solution)/shard_map/convert_element_type | solution.py:65
  83.1 3.3 %collective-permute-start.6 = (bf16[2,384,256]{1,2,0:T(8,128)(2,1)}, bf16[2,384,256]{1,2,0:T(8,128)(2,1)S(1)}, u32[]{:S(2)}, u32[]{:S(2)}) collective-permute-start(bf16[2,384,256]{1,2,0:T(8,128)(2,1)} %gather_fusion.7), channel_id=1, source_target_pairs={{0,1},{1,2},{2,3},{3,4},{4,5},{5,6},{6,7},{7,8},{8,9},{9,10},{10,1... | collective-permute-start | bytes 1179656 | tf_op jit(solution)/shard_map/ppermute | solution.py:12
  86.4 4.9 %collective-permute-start.7 = (bf16[2,384,256]{1,2,0:T(8,128)(2,1)}, bf16[2,384,256]{1,2,0:T(8,128)(2,1)S(1)}, u32[]{:S(2)}, u32[]{:S(2)}) collective-permute-start(bf16[2,384,256]{1,2,0:T(8,128)(2,1)} %gather_fusion.8), channel_id=1, source_target_pairs={{0,2},{1,3},{2,4},{3,5},{4,6},{5,7},{6,8},{7,9},{8,10},{9,11},{10,... | collective-permute-start | bytes 1179656 | tf_op jit(solution)/shard_map/ppermute | solution.py:12
  91.3 3.4 %multiply_reduce_fusion.1 = f32[8,128,256]{2,1,0:T(8,128)} fusion(f32[8,3,128,256]{3,2,1,0:T(8,128)} %bitcast.51, f32[8,3,128]{2,1,0:T(4,128)} %copy.19), kind=kLoop, calls=%fused_computation.27 | loop fusion | flops 1310720 | bytes 4206592 | tf_op jit(solution)/shard_map/reduce_sum | solution.py:68
  94.7 1.1 constant_dynamic-update-slice_fusion.8
  95.8 0.1 constant_dynamic-update-slice_fusion.7
  95.9 0.1 constant_dynamic-update-slice_fusion.6
  95.9 5.0 %collective-permute-done.7 = bf16[2,384,256]{1,2,0:T(8,128)(2,1)S(1)} collective-permute-done((bf16[2,384,256]{1,2,0:T(8,128)(2,1)}, bf16[2,384,256]{1,2,0:T(8,128)(2,1)S(1)}, u32[]{:S(2)}, u32[]{:S(2)}) %collective-permute-start.7) | collective-permute-done | bytes 393248 | tf_op jit(solution)/shard_map/ppermute | solution.py:12
  100.9 0.1 constant_dynamic-update-slice_fusion.5
  101.0 6.8 %gather_fusion.9 = bf16[48,384,256]{1,2,0:T(8,128)(2,1)} fusion(bf16[16,384,256]{1,2,0:T(8,128)(2,1)S(1)} %constant_dynamic-update-slice_fusion.5, s32[1024]{0:T(1024)} %copy-done.2), kind=kCustom, calls=%fused_computation.9 | custom fusion | bytes 18874560 | tf_op jit(solution)/shard_map/gather | solution.py:27
  107.8 16.3 %fusion.10 = bf16[8,384,256]{1,2,0:T(8,128)(2,1)} fusion(f32[8,128,256]{1,2,0:T(8,128)} %get-tuple-element.15, bf16[8,6,384,384]{3,2,1,0:T(8,128)(2,1)} %param.11, bf16[8,6,384,256]{2,3,1,0:T(8,128)(2,1)} %bitcast.53, pred[8,6]{1,0:T(8,128)(4,1)S(1)} %copy-done.16, f32[8,384]{1,0:T(8,128)S(1)} %copy-done.5, bf16[8,384,256]{1,2,0:T(8,128)(2,1)} %get-tuple-element.19), kind=kOutput, calls=%fused_computation.21 | convolution fusion | flops 3632529408 | bytes 27799600 | tf_op jit(solution)/shard_map/bkij,bkjf->bif/dot_general | solution.py:29
  124.2 1.7 copy.22
  125.9 2.6 %copy.23 = bf16[8,384,256]{2,1,0:T(8,128)(2,1)} copy(bf16[8,384,256]{1,2,0:T(8,128)(2,1)} %fusion.10) | data formatting | bytes 3145728
  128.5 0.5 multiply_reduce_fusion
  128.9 0.7 copy-done.1
  129.7 0.2 multiply_reduce_fusion.2
  129.9 81.4 %psum.7 = f32[256]{0:T(256)S(1)} all-reduce(f32[256]{0:T(256)S(1)} %get-tuple-element.10), channel_id=1, replica_groups=mesh['dom'=128] {'dom'}, use_global_device_ids=true, to_apply=%region_3.4 | all-reduce | flops 256 | bytes 2048 | tf_op jit(solution)/shard_map/psum | solution.py:71
  211.3 1.1 broadcast_multiply_fusion
  (53 shorter events, 0.2 us)
Async XLA Ops:
  0.6 23.1 %copy-start.3 = (s32[8,6]{1,0:T(8,128)S(1)}, s32[8,6]{1,0:T(8,128)}, u32[]{:S(2)}) copy-start(s32[8,6]{1,0:T(8,128)} %param.12) | copy-start | bytes 580
  0.6 23.1 %copy-start.10 = (s32[8,128]{1,0:T(8,128)S(1)}, s32[8,128]{1,0:T(8,128)}, u32[]{:S(2)}) copy-start(s32[8,128]{1,0:T(8,128)} %param.14) | copy-start | bytes 12292
  0.7 23.1 %copy-start.13 = (s32[256]{0:T(256)S(1)}, s32[256]{0:T(256)}, u32[]{:S(2)}) copy-start(s32[256]{0:T(256)} %param.16) | copy-start | bytes 3076
  0.7 23.1 %copy-start.14 = (s32[256]{0:T(256)S(1)}, s32[256]{0:T(256)}, u32[]{:S(2)}) copy-start(s32[256]{0:T(256)} %param.17) | copy-start | bytes 3076
  0.7 23.1 %copy-start.12 = (f32[256]{0:T(256)S(1)}, f32[256]{0:T(256)}, u32[]{:S(2)}) copy-start(f32[256]{0:T(256)} %param.18) | copy-start | bytes 3076
  0.7 23.1 %copy-start.11 = (s32[256]{0:T(256)S(1)}, s32[256]{0:T(256)}, u32[]{:S(2)}) copy-start(s32[256]{0:T(256)} %param.15) | copy-start | bytes 3076
  1.8 21.9 %copy-start.6 = (s32[1024]{0:T(1024)}, s32[1024]{0:T(1024)S(1)}, u32[]{:S(2)}) copy-start(s32[1024]{0:T(1024)S(1)} %pad_clamp_fusion.4) | copy-start | bytes 12292
  4.5 25.5 %collective-permute-start = (bf16[2,384,256]{2,1,0:T(8,128)(2,1)}, bf16[2,384,256]{2,1,0:T(8,128)(2,1)S(1)}, u32[]{:S(2)}, u32[]{:S(2)}) collective-permute-start(bf16[2,384,256]{2,1,0:T(8,128)(2,1)} %gather_fusion), channel_id=1, source_target_pairs={{2,0},{3,1},{4,2},{5,3},{6,4},{7,5},{8,6},{9,7},{10,8},{11,9},{12,... | collective-permute-start | bytes 1179656 | tf_op jit(solution)/shard_map/ppermute | solution.py:12
  5.8 4.0 %copy-start.8 = (s32[1024]{0:T(1024)}, s32[1024]{0:T(1024)S(1)}, u32[]{:S(2)}) copy-start(s32[1024]{0:T(1024)S(1)} %pad_clamp_fusion.3) | copy-start | bytes 12292
  8.5 21.5 %collective-permute-start.1 = (bf16[2,384,256]{2,1,0:T(8,128)(2,1)}, bf16[2,384,256]{2,1,0:T(8,128)(2,1)}, u32[]{:S(2)}, u32[]{:S(2)}) collective-permute-start(bf16[2,384,256]{2,1,0:T(8,128)(2,1)} %gather_fusion.1), channel_id=1, source_target_pairs={{1,0},{2,1},{3,2},{4,3},{5,4},{6,5},{7,6},{8,7},{9,8},{10,9},{11,1... | collective-permute-start | bytes 1179656 | tf_op jit(solution)/shard_map/ppermute | solution.py:12
  9.8 15.6 %copy-start.7 = (s32[1024]{0:T(1024)}, s32[1024]{0:T(1024)S(1)}, u32[]{:S(2)}) copy-start(s32[1024]{0:T(1024)S(1)} %pad_clamp_fusion.2) | copy-start | bytes 12292
  12.6 18.4 %collective-permute-start.2 = (bf16[2,384,256]{2,1,0:T(8,128)(2,1)}, bf16[2,384,256]{2,1,0:T(8,128)(2,1)}, u32[]{:S(2)}, u32[]{:S(2)}) collective-permute-start(bf16[2,384,256]{2,1,0:T(8,128)(2,1)} %gather_fusion.2), channel_id=1, source_target_pairs={{0,1},{1,2},{2,3},{3,4},{4,5},{5,6},{6,7},{7,8},{8,9},{9,10},{10,1... | collective-permute-start | bytes 1179656 | tf_op jit(solution)/shard_map/ppermute | solution.py:12
  16.4 9.0 %copy-start.9 = (s32[1024]{0:T(1024)}, s32[1024]{0:T(1024)S(1)}, u32[]{:S(2)}) copy-start(s32[1024]{0:T(1024)S(1)} %pad_clamp_fusion.1) | copy-start | bytes 12292
  19.1 13.3 %collective-permute-start.3 = (bf16[2,384,256]{2,1,0:T(8,128)(2,1)}, bf16[2,384,256]{2,1,0:T(8,128)(2,1)}, u32[]{:S(2)}, u32[]{:S(2)}) collective-permute-start(bf16[2,384,256]{2,1,0:T(8,128)(2,1)} %gather_fusion.3), channel_id=1, source_target_pairs={{0,2},{1,3},{2,4},{3,5},{4,6},{5,7},{6,8},{7,9},{8,10},{9,11},{10,... | collective-permute-start | bytes 1179656 | tf_op jit(solution)/shard_map/ppermute | solution.py:12
  23.7 2.3 %copy-start = (bf16[8,384,256]{2,1,0:T(8,128)(2,1)S(1)}, bf16[8,384,256]{2,1,0:T(8,128)(2,1)}, u32[]{:S(2)}) copy-start(bf16[8,384,256]{2,1,0:T(8,128)(2,1)} %param.10) | copy-start | bytes 4718596
  23.8 28.6 %copy-start.4 = (f32[8,384]{1,0:T(8,128)}, f32[8,384]{1,0:T(8,128)S(1)}, u32[]{:S(2)}) copy-start(f32[8,384]{1,0:T(8,128)S(1)} %broadcast_bitcast_fusion) | copy-start | bytes 36868
  27.4 6.0 %copy-start.2 = (s32[1024]{0:T(1024)}, s32[1024]{0:T(1024)S(1)}, u32[]{:S(2)}) copy-start(s32[1024]{0:T(1024)S(1)} %pad_clamp_fusion) | copy-start | bytes 12292
  39.7 12.6 %copy-start.15 = (pred[8,6]{1,0:T(8,128)(4,1)S(1)}, pred[8,6]{1,0:T(8,128)(4,1)}, u32[]{:S(2)}) copy-start(pred[8,6]{1,0:T(8,128)(4,1)} %broadcast_compare_fusion) | copy-start | bytes 148
  70.3 24.4 %collective-permute-start.4 = (bf16[2,384,256]{1,2,0:T(8,128)(2,1)}, bf16[2,384,256]{1,2,0:T(8,128)(2,1)}, u32[]{:S(2)}, u32[]{:S(2)}) collective-permute-start(bf16[2,384,256]{1,2,0:T(8,128)(2,1)} %gather_fusion.5), channel_id=1, source_target_pairs={{2,0},{3,1},{4,2},{5,3},{6,4},{7,5},{8,6},{9,7},{10,8},{11,9},{12,... | collective-permute-start | bytes 1179656 | tf_op jit(solution)/shard_map/ppermute | solution.py:12
  71.6 24.2 %collective-permute-start.5 = (bf16[2,384,256]{1,2,0:T(8,128)(2,1)}, bf16[2,384,256]{1,2,0:T(8,128)(2,1)S(1)}, u32[]{:S(2)}, u32[]{:S(2)}) collective-permute-start(bf16[2,384,256]{1,2,0:T(8,128)(2,1)} %gather_fusion.6), channel_id=1, source_target_pairs={{1,0},{2,1},{3,2},{4,3},{5,4},{6,5},{7,6},{8,7},{9,8},{10,9},{11,1... | collective-permute-start | bytes 1179656 | tf_op jit(solution)/shard_map/ppermute | solution.py:12
  83.1 12.8 %collective-permute-start.6 = (bf16[2,384,256]{1,2,0:T(8,128)(2,1)}, bf16[2,384,256]{1,2,0:T(8,128)(2,1)S(1)}, u32[]{:S(2)}, u32[]{:S(2)}) collective-permute-start(bf16[2,384,256]{1,2,0:T(8,128)(2,1)} %gather_fusion.7), channel_id=1, source_target_pairs={{0,1},{1,2},{2,3},{3,4},{4,5},{5,6},{6,7},{7,8},{8,9},{9,10},{10,1... | collective-permute-start | bytes 1179656 | tf_op jit(solution)/shard_map/ppermute | solution.py:12
  86.4 14.5 %collective-permute-start.7 = (bf16[2,384,256]{1,2,0:T(8,128)(2,1)}, bf16[2,384,256]{1,2,0:T(8,128)(2,1)S(1)}, u32[]{:S(2)}, u32[]{:S(2)}) collective-permute-start(bf16[2,384,256]{1,2,0:T(8,128)(2,1)} %gather_fusion.8), channel_id=1, source_target_pairs={{0,2},{1,3},{2,4},{3,5},{4,6},{5,7},{6,8},{7,9},{8,10},{9,11},{10,... | collective-permute-start | bytes 1179656 | tf_op jit(solution)/shard_map/ppermute | solution.py:12
  101.0 6.8 %copy-start.5 = (f32[8,384]{1,0:T(8,128)S(1)}, f32[8,384]{1,0:T(8,128)}, u32[]{:S(2)}) copy-start(f32[8,384]{1,0:T(8,128)} %copy-done.4) | copy-start | bytes 36868
  101.0 6.8 %copy-start.16 = (pred[8,6]{1,0:T(8,128)(4,1)S(1)}, pred[8,6]{1,0:T(8,128)(4,1)}, u32[]{:S(2)}) copy-start(pred[8,6]{1,0:T(8,128)(4,1)} %broadcast_compare_fusion) | copy-start | bytes 148
  128.4 1.2 copy-start.1
where the time goes:
time: 214 us; the launch traced here: 212 us
  blocking collectives  81.4 us (38%)
  local copies, waits for them, and re-layouts  65.3 us (31%)
  matrix products  28.6 us (13%)
  starting transfers between devices  21.7 us (10%)
  other arithmetic  9.13 us (4%)
  waiting for transfers between devices  5.31 us (2%)
    psum x1, blocking collectives, per_device(): totals = lax.psum(jnp.sum(raw * raw, axis=(0, 1)), 'dom')  81.4 us
    dot_general x2, matrix products, coupled_rows(): jnp.einsum('bkij,bkjf->bif', operator_blocks, picked, preferred_element_t...  28.6 us
    gather x3, local copies, waits for them, and re-layouts, coupled_rows(): picked = extended[jnp.clip(block_cols, 0, last)]  25.7 us
    gather x8, local copies, waits for them, and re-layouts, extended_state(): adjoint[jnp.clip(send_lists[group], 0, owned - 1)]  22.4 us
    ppermute x8, starting transfers between devices, passed_along(): return lax.ppermute(value, axis, pairs)  21.7 us
    unnamed x43, local copies, waits for them, and re-layouts  9.34 us
    ppermute x8, waiting for transfers between devices, passed_along(): return lax.ppermute(value, axis, pairs)  5.31 us
  transfers between devices with their start and end apart: 8, of which 2 were waited for; matrix products, arithmetic and copies ran while one was open for 15% of the time, Pallas kernels for 0%

commit v1 on v0

v1 whole, which is shorter than its diff:
```python
import functools

import jax
import jax.numpy as jnp
from jax import lax
from jax.experimental import pallas as pl
from jax.experimental.pallas import tpu as pltpu
from jax.sharding import PartitionSpec as P

neighbour_offsets = (-2, -1, 1, 2)
MESH = pl.DeviceIdType.MESH
LANES = 128
STEPS = 2


def kernel(
    devices,
    line,
    adj_hbm,
    ops_hbm,
    cols_hbm,
    lists_hbm,
    wet_hbm,
    cells_hbm,
    first_hbm,
    length_hbm,
    gain_hbm,
    snap_hbm,
    adj_out,
    sens_out,
    *scratch,
):
    names = iter(scratch)
    take = lambda n: [next(names) for _ in range(n)]
    (ops,) = take(1)
    ext = [take(2), take(2)]
    own = [take(2), take(2)]
    sent = [take(2), take(2)]
    final = take(2)
    raw = take(2)
    sens = take(2)
    snap_b, wet_b = take(2)
    columns_m, cols, lists = take(3)
    functional = take(4)
    mine = take(2)
    line_sum = take(2)
    from_line = take(2)
    from_plane = take(2)
    in_sem, ops_sem, send_sem, recv_sem, line_send, line_recv, plane_send, plane_recv, out_sem = take(9)

    owned, rows = own[0][0].shape[0], own[0][0].shape[1]
    entries = ops.shape[1]
    cells = rows // 3
    capacity = 2
    me = lax.axis_index("dom")
    planes = devices // line

    loads = []

    def load(src, dst):
        copy = pltpu.make_async_copy(src, dst, in_sem.at[len(loads)])
        copy.start()
        loads.append(copy)
        return copy

    lists_in = load(lists_hbm, lists)
    adj_in = []
    for h in range(2):
        half = adj_hbm.at[:, :, pl.ds(h * LANES, LANES)]
        adj_in.append(load(half, own[0][h]))
    ext_in = []
    for h in range(2):
        half = adj_hbm.at[:, :, pl.ds(h * LANES, LANES)]
        ext_in.append(load(half, ext[0][h].at[pl.ds(0, owned)]))
    small_in = [load(cols_hbm, cols)]
    for s in range(STEPS):
        for c in range(3):
            small_in.append(
                load(
                    snap_hbm.at[s, :, pl.ds(c * cells, cells)],
                    columns_m.at[pl.ds((s * 3 + c) * owned, owned)],
                )
            )
    for src, dst in zip((cells_hbm, first_hbm, length_hbm, gain_hbm), functional[:4]):
        small_in.append(load(src, dst))
    wet_i = next(names)
    small_in.append(load(wet_hbm, wet_i))
    ops_in = []
    for b in range(owned):
        copy = pltpu.make_async_copy(ops_hbm.at[b], ops.at[b], ops_sem.at[b])
        copy.start()
        ops_in.append(copy)

    barrier = pltpu.get_barrier_semaphore()
    greeted = jnp.int32(line - 1 + planes - 1)
    exists = []
    for offset in neighbour_offsets:
        target = me + offset
        there = (target >= 0) & (target < devices)
        exists.append(there)
        greeted = greeted + there.astype(jnp.int32)

        @pl.when(there)
        def _():
            pl.semaphore_signal(barrier, inc=1, device_id=(target,), device_id_type=MESH)

    def line_peer(j):
        return (me // line) * line + lax.rem(me + j, line)

    def plane_peer(j):
        return lax.rem(me + j * line, devices)

    for j in range(1, line):
        pl.semaphore_signal(barrier, inc=1, device_id=(line_peer(j),), device_id_type=MESH)
    for j in range(1, planes):
        pl.semaphore_signal(barrier, inc=1, device_id=(plane_peer(j),), device_id_type=MESH)

    for s in range(STEPS):
        for h in range(2):
            ext[s][h][2 * owned] = jnp.zeros((rows, LANES), jnp.bfloat16)

    def halo_copy(s, h, group):
        return pltpu.make_async_remote_copy(
            src_ref=sent[s][h].at[pl.ds(group * capacity, capacity)],
            dst_ref=ext[s][h].at[pl.ds(owned + group * capacity, capacity)],
            send_sem=send_sem.at[s, h, group],
            recv_sem=recv_sem.at[s, h, group],
            device_id=(jnp.clip(me + neighbour_offsets[group], 0, devices - 1),),
            device_id_type=MESH,
        )

    def gather(s, h):
        for group in range(4):
            for c in range(capacity):
                block = jnp.maximum(lists[0, group, c], 0)
                sent[s][h][group * capacity + c] = own[s][h][block]

    def send(s, h):
        for group in (0, 3, 1, 2):

            @pl.when(exists[group])
            def _():
                halo_copy(s, h, group).start()

    def await_halo(s, h):
        for group in range(4):

            @pl.when(exists[3 - group])
            def _():
                halo_copy(s, h, group).wait_recv()

    lists_in.wait()
    adj_in[0].wait()
    gather(0, 0)
    pl.semaphore_wait(barrier, greeted)
    send(0, 0)
    adj_in[1].wait()
    gather(0, 1)
    send(0, 1)

    for copy in small_in:
        copy.wait()
    used = 2 * 3 * owned
    columns_m[pl.ds(used, owned)] = wet_i[...].astype(jnp.float32)
    turned = jnp.transpose(columns_m[...])
    for s in range(STEPS):
        for c in range(3):
            for b in range(owned):
                at = (s * 3 + c) * owned + b
                snap_b[s, b, pl.ds(c * cells, cells)] = jnp.broadcast_to(
                    turned[:, at : at + 1], (cells, LANES)
                )
    for b in range(owned):
        at = used + b
        wet_b[b] = jnp.broadcast_to(turned[:, at : at + 1], (cells, LANES))

    for copy in ext_in:
        copy.wait()
    for copy in ops_in:
        copy.wait()

    row_in_block = lax.broadcasted_iota(jnp.int32, (cells, LANES), 0)

    def advance(s, h):
        part = pl.ds(h * LANES, LANES)
        at_cell = functional[0][:, part]
        first = functional[1][:, part]
        active = jnp.where(
            (first <= s) & (s < first + functional[2][:, part]), functional[3][:, part], 0.0
        )

        def one_row(b, squares):
            picked = []
            for k in range(entries):
                col = cols[b, k]
                picked.append(ext[s][h][jnp.where(col < 0, 2 * owned, col)])
            coupled = jnp.dot(
                jnp.concatenate([ops[b, k] for k in range(entries)], axis=1),
                jnp.concatenate(picked, axis=0),
                preferred_element_type=jnp.float32,
            )
            wet = wet_b[b]
            here = row_in_block + (me * owned + b) * cells
            source = jnp.where(here == at_cell, active, 0.0)
            total = None
            for c in range(3):
                piece = slice(c * cells, (c + 1) * cells)
                now = own[s][h][b, piece].astype(jnp.float32)
                updated = wet * (now + coupled[piece])
                if c == 0:
                    updated = updated + source
                rounded = updated.astype(jnp.bfloat16)
                if s + 1 < STEPS:
                    own[s + 1][h][b, piece] = rounded
                    ext[s + 1][h][b, piece] = rounded
                else:
                    final[h][b, piece] = rounded
                term = snap_b[s, b, piece] * rounded.astype(jnp.float32)
                total = term if total is None else total + term
            if s > 0:
                total = raw[h][b] + total
            raw[h][b] = total
            if s + 1 < STEPS:
                return squares
            return squares + jnp.sum((total * total).reshape(cells // 8, 8, LANES), axis=0)

        return lax.fori_loop(0, owned, one_row, jnp.zeros((8, LANES), jnp.float32))

    def line_copy(h, j):
        return pltpu.make_async_remote_copy(
            src_ref=mine[h],
            dst_ref=from_line[h].at[j - 1],
            send_sem=line_send.at[h, j - 1],
            recv_sem=line_recv.at[h, j - 1],
            device_id=(line_peer(j),),
            device_id_type=MESH,
        )

    def plane_copy(h, j):
        return pltpu.make_async_remote_copy(
            src_ref=line_sum[h],
            dst_ref=from_plane[h].at[j - 1],
            send_sem=plane_send.at[h, j - 1],
            recv_sem=plane_recv.at[h, j - 1],
            device_id=(plane_peer(j),),
            device_id_type=MESH,
        )

    def reduce_line_start(h, squares):
        mine[h][...] = jnp.sum(squares, axis=0, keepdims=True)
        for j in range(1, line):
            line_copy(h, j).start()

    def reduce_plane_start(h):
        total = mine[h][...]
        for j in range(1, line):
            line_copy(h, j).wait_recv()
            total = total + from_line[h][j - 1]
        line_sum[h][...] = total
        for j in range(1, planes):
            plane_copy(h, j).start()

    def finish(h):
        total = line_sum[h][...]
        for j in range(1, planes):
            plane_copy(h, j).wait_recv()
            total = total + from_plane[h][j - 1]
        meansq = total / (devices * owned * cells)
        scale = lax.rsqrt(meansq + 1e-6)
        for b in range(owned):
            sens[h][b] = raw[h][b] * scale
        copy = pltpu.make_async_copy(
            sens[h], sens_out.at[:, :, pl.ds(h * LANES, LANES)], out_sem.at[1, h]
        )
        copy.start()
        return copy

    def put_final(h):
        copy = pltpu.make_async_copy(
            final[h], adj_out.at[:, :, pl.ds(h * LANES, LANES)], out_sem.at[0, h]
        )
        copy.start()
        return copy

    for h in range(2):
        await_halo(0, h)
        advance(0, h)
        gather(1, h)
        send(1, h)

    puts = []
    await_halo(1, 0)
    squares = advance(1, 0)
    reduce_line_start(0, squares)
    puts.append(put_final(0))
    await_halo(1, 1)
    reduce_plane_start(0)
    squares = advance(1, 1)
    reduce_line_start(1, squares)
    puts.append(put_final(1))
    puts.append(finish(0))
    reduce_plane_start(1)
    puts.append(finish(1))

    for s in range(STEPS):
        for h in range(2):
            for group in range(4):

                @pl.when(exists[group])
                def _():
                    halo_copy(s, h, group).wait_send()

    for h in range(2):
        for j in range(1, line):
            line_copy(h, j).wait_send()
        for j in range(1, planes):
            plane_copy(h, j).wait_send()
    for copy in puts:
        copy.wait()


def per_device(
    adjoint_end,
    operator_blocks,
    block_cols,
    halo_send,
    wet_cells,
    gauge_cells,
    window_first,
    window_len,
    gauge_gain,
    snapshots,
):
    devices = lax.axis_size("dom")
    owned, rows, width = adjoint_end.shape
    entries = operator_blocks.shape[1]
    cells = rows // 3
    line = 8
    bf16, f32, i32 = jnp.bfloat16, jnp.float32, jnp.int32
    slots = 2 * owned + 1
    scratch = (
        [pltpu.VMEM((owned, entries, rows, rows), bf16)]
        + [pltpu.VMEM((slots, rows, LANES), bf16)] * 4
        + [pltpu.VMEM((owned, rows, LANES), bf16)] * 4
        + [pltpu.VMEM((owned, rows, LANES), bf16)] * 4
        + [pltpu.VMEM((owned, rows, LANES), bf16)] * 2
        + [pltpu.VMEM((owned, cells, LANES), f32)] * 2
        + [pltpu.VMEM((owned, cells, LANES), f32)] * 2
        + [
            pltpu.VMEM((STEPS, owned, rows, LANES), f32),
            pltpu.VMEM((owned, cells, LANES), f32),
            pltpu.VMEM((LANES, LANES), f32),
            pltpu.SMEM(block_cols.shape, i32),
            pltpu.SMEM(halo_send.shape, i32),
        ]
        + [pltpu.VMEM((1, width), i32)] * 3
        + [pltpu.VMEM((1, width), f32)]
        + [pltpu.VMEM((1, LANES), f32)] * 4
        + [pltpu.VMEM((line - 1, 1, LANES), f32)] * 2
        + [pltpu.VMEM((devices // line - 1, 1, LANES), f32)] * 2
        + [
            pltpu.SemaphoreType.DMA((17,)),
            pltpu.SemaphoreType.DMA((owned,)),
            pltpu.SemaphoreType.DMA((STEPS, 2, 4)),
            pltpu.SemaphoreType.DMA((STEPS, 2, 4)),
            pltpu.SemaphoreType.DMA((2, line - 1)),
            pltpu.SemaphoreType.DMA((2, line - 1)),
            pltpu.SemaphoreType.DMA((2, devices // line - 1)),
            pltpu.SemaphoreType.DMA((2, devices // line - 1)),
            pltpu.SemaphoreType.DMA((2, 2)),
            pltpu.VMEM(wet_cells.shape, i32),
        ]
    )
    anywhere = pl.BlockSpec(memory_space=pl.ANY)
    row = lambda v: v.reshape(1, width)
    return pl.pallas_call(
        functools.partial(kernel, devices, line),
        out_shape=(
            jax.ShapeDtypeStruct(adjoint_end.shape, bf16),
            jax.ShapeDtypeStruct((owned, cells, width), f32),
        ),
        in_specs=[anywhere] * 10,
        out_specs=(anywhere, anywhere),
        scratch_shapes=scratch,
        compiler_params=pltpu.CompilerParams(
            collective_id=0, has_side_effects=True, vmem_limit_bytes=56 * 1024 * 1024
        ),
        name="adjoint",
    )(
        adjoint_end,
        operator_blocks,
        block_cols,
        halo_send,
        wet_cells,
        row(gauge_cells),
        row(window_first),
        row(window_len),
        row(gauge_gain),
        snapshots,
    )


def solution(mesh):
    return jax.shard_map(
        per_device,
        mesh=mesh,
        in_specs=(
            P("dom", None, None),
            P("dom", None, None, None),
            P("dom", None),
            P("dom", None, None),
            P("dom", None),
            P(),
            P(),
            P(),
            P(),
            P(None, "dom", None),
        ),
        out_specs=(P("dom", None, None), P("dom", None, None)),
        check_vma=False,
    )
```

time: 214 us -> 62.8 us (0.29)
  blocking collectives: 81.4 us -> 0 us
  local copies, waits for them, and re-layouts: 65.3 us -> 5.05 us
  Pallas kernels: 0 us -> 57 us
  matrix products: 28.6 us -> 0 us
  starting transfers between devices: 21.7 us -> 0 us
  other arithmetic: 9.13 us -> 0 us
  waiting for transfers between devices: 5.31 us -> 0 us
    psum x1 -> x0, blocking collectives: 81.4 us -> none  [per_device(): totals = lax.psum(jnp.sum(raw * raw, axis=(0, 1)), 'dom')]
    pallas_call x0 -> x1, Pallas kernels: none -> 57 us  [per_device(): pl.pallas_call(functools.partial(kernel, devices, line), out_shape=(jax.S...]
    gather x11 -> x0, local copies, waits for them, and re-layouts: 48.2 us -> none  [the longest x3 25.7 us: coupled_rows(): picked = extended[jnp.clip(block_cols, 0, last)]]
    dot_general x2 -> x0, matrix products: 28.6 us -> none  [coupled_rows(): jnp.einsum('bkij,bkjf->bif', operator_blocks, picked, preferred_element_t...]
    ppermute x8 -> x0, starting transfers between devices: 21.7 us -> none  [passed_along(): return lax.ppermute(value, axis, pairs)]
    ppermute x8 -> x0, waiting for transfers between devices: 5.31 us -> none  [passed_along(): return lax.ppermute(value, axis, pairs)]
    unnamed x43 -> x5, local copies, waits for them, and re-layouts: 9.34 us -> 5.05 us
    reduce_sum x3 -> x0, other arithmetic: 4.11 us -> none  [the longest x2 3.87 us: per_device(): jnp.sum(saved * adjoint.astype(jnp.float32).reshape(owned, 3, cell_count,...]
  transfers between devices with their start and end apart: 8 -> 0, of which waited for: 2 -> 0; matrix products, arithmetic and copies ran while one was open for 15% -> 0% of each run, Pallas kernels for 0% -> 0%
where the time goes in v1:
time: 62.8 us; the launch traced here: 62.7 us
  Pallas kernels  57 us (91%)
  local copies, waits for them, and re-layouts  5.05 us (8%)
  between operations  0.65 us (1%)
    pallas_call x1, Pallas kernels, per_device(): pl.pallas_call(functools.partial(kernel, devices, line), out_shape=(jax.S...  57 us
    unnamed x5, local copies, waits for them, and re-layouts  5.05 us

profile of v1, /device:TPU:0, one launch (start us, length us, event | category | flops | bytes accessed | tf_op | source)
XLA Modules:
  0.0 62.7 jit_solution(7281681605321012417)
XLA Ops:
  0.6 1.3 %copy.12.lists_hbm = s32[1,4,2]{2,1,0:T(4,128)} copy(s32[1,4,2]{1,2,0:T(2,128)} %param.13) | data formatting | bytes 64 | tf_op args[3]
  2.0 57.0 %adjoint.1 = (bf16[8,384,256]{2,1,0:T(8,128)(2,1)}, f32[8,128,256]{2,1,0:T(8,128)}) custom-call(bf16[8,384,256]{2,1,0:T(8,128)(2,1)} %adj_hbm.1, bf16[8,6,384,384]{3,2,1,0:T(8,128)(2,1)} %ops_hbm.1, s32[8,6]{1,0:T(8,128)} %cols_hbm.1, s32[1,4,2]{2,1,0:T(4,128)} %copy.12.lists_hbm, s32[8,128]{1,0:T(8,128)} %wet_hbm.1, s32[1,256]{1,0:T(1,128)} %bitcast.4, ...), custom_call_target="tpu_custom_call" | custom-call | tf_op jit(solution)/shard_map/adjoint/pallas_call | solution.py:376
  58.9 0.0 copy-start
  58.9 2.7 %copy.15 = bf16[8,384,256]{2,1,0:T(8,128)(2,1)} copy(bf16[8,384,256]{2,1,0:T(8,128)(2,1)} %get-tuple-element.4) | data formatting | bytes 3145728
  61.7 0.0 copy-done
  61.7 1.0 %copy.16 = f32[8,128,256]{2,1,0:T(8,128)} copy(f32[8,128,256]{2,1,0:T(8,128)S(1)} %copy-done) | data formatting | bytes 2097152
Async XLA Ops:
  58.9 2.8 %copy-start = (f32[8,128,256]{2,1,0:T(8,128)S(1)}, f32[8,128,256]{2,1,0:T(8,128)}, u32[]{:S(2)}) copy-start(f32[8,128,256]{2,1,0:T(8,128)} %get-tuple-element.5) | copy-start | bytes 3145732

commit v2 on v1

--- a/solution.py
+++ b/solution.py
@@ -11,6 +11,8 @@
 MESH = pl.DeviceIdType.MESH
 LANES = 128
 STEPS = 2
+UNROLL = 4
+VM = 44
 
 
 def kernel(
@@ -132,13 +134,20 @@
     def gather(s, h):
         for group in range(4):
             for c in range(capacity):
-                block = jnp.maximum(lists[0, group, c], 0)
+                block = jnp.maximum(lists[0, c, group], 0)
                 sent[s][h][group * capacity + c] = own[s][h][block]
 
-    def send(s, h):
+    odd = lax.rem(me, 2)
+    light = (odd == 1, False, False, odd == 0)
+
+    def send(s, h, which=None):
         for group in (0, 3, 1, 2):
-
-            @pl.when(exists[group])
+            go = exists[group]
+            if which is not None:
+                held = jnp.logical_and(light[group], go)
+                go = held if which == "held" else jnp.logical_and(jnp.logical_not(light[group]), go)
+
+            @pl.when(go)
             def _():
                 halo_copy(s, h, group).start()
 
@@ -156,7 +165,7 @@
     send(0, 0)
     adj_in[1].wait()
     gather(0, 1)
-    send(0, 1)
+    send(0, 1, "first")
 
     for copy in small_in:
         copy.wait()
@@ -224,7 +233,7 @@
                 return squares
             return squares + jnp.sum((total * total).reshape(cells // 8, 8, LANES), axis=0)
 
-        return lax.fori_loop(0, owned, one_row, jnp.zeros((8, LANES), jnp.float32))
+        return lax.fori_loop(0, owned, one_row, jnp.zeros((8, LANES), jnp.float32), unroll=UNROLL)
 
     def line_copy(h, j):
         return pltpu.make_async_remote_copy(
@@ -284,6 +293,8 @@
 
     for h in range(2):
         await_halo(0, h)
+        if h == 0:
+            send(0, 1, "held")
         advance(0, h)
         gather(1, h)
         send(1, h)
@@ -351,7 +362,7 @@
             pltpu.VMEM((owned, cells, LANES), f32),
             pltpu.VMEM((LANES, LANES), f32),
             pltpu.SMEM(block_cols.shape, i32),
-            pltpu.SMEM(halo_send.shape, i32),
+            pltpu.SMEM((1, 2, 4), i32),
         ]
         + [pltpu.VMEM((1, width), i32)] * 3
         + [pltpu.VMEM((1, width), f32)]
@@ -373,6 +384,7 @@
     )
     anywhere = pl.BlockSpec(memory_space=pl.ANY)
     row = lambda v: v.reshape(1, width)
+    turned_lists = jnp.swapaxes(halo_send, 1, 2)
     return pl.pallas_call(
         functools.partial(kernel, devices, line),
         out_shape=(
@@ -383,20 +395,11 @@
         out_specs=(anywhere, anywhere),
         scratch_shapes=scratch,
         compiler_params=pltpu.CompilerParams(
-            collective_id=0, has_side_effects=True, vmem_limit_bytes=56 * 1024 * 1024
+            collective_id=0, has_side_effects=True, vmem_limit_bytes=VM * 1024 * 1024
         ),
         name="adjoint",
     )(
-        adjoint_end,
-        operator_blocks,
-        block_cols,
-        halo_send,
-        wet_cells,
-        row(gauge_cells),
-        row(window_first),
-        row(window_len),
-        row(gauge_gain),
-        snapshots,
+        *(pltpu.with_memory_space_constraint(v, pltpu.HBM) for v in (adjoint_end, operator_blocks, block_cols, turned_lists, wet_cells, row(gauge_cells), row(window_first), row(window_len), row(gauge_gain), snapshots))
     )
 
 

time: 62.8 us -> 54.5 us (0.87)
  Pallas kernels: 57 us -> 51.7 us
  local copies, waits for them, and re-layouts: 5.05 us -> 2.11 us
    pallas_call x1, Pallas kernels: 57 us -> 51.7 us  [per_device(): pl.pallas_call(functools.partial(kernel, devices, line), out_shape=(jax.S...]
    unnamed x5 -> x2, local copies, waits for them, and re-layouts: 5.05 us -> 2.11 us
where the time goes in v2:
time: 54.5 us; the launch traced here: 54.4 us
  Pallas kernels  51.7 us (95%)
  local copies, waits for them, and re-layouts  2.11 us (4%)
  between operations  0.64 us (1%)
    pallas_call x1, Pallas kernels, per_device(): pl.pallas_call(functools.partial(kernel, devices, line), out_shape=(jax.S...  51.7 us
    unnamed x2, local copies, waits for them, and re-layouts  2.11 us

profile of v2, /device:TPU:0, one launch (start us, length us, event | category | flops | bytes accessed | tf_op | source)
XLA Modules:
  0.0 54.4 jit_solution(924966350994027496)
XLA Ops:
  0.6 51.7 %adjoint.1 = (bf16[8,384,256]{2,1,0:T(8,128)(2,1)S(1)}, f32[8,128,256]{2,1,0:T(8,128)S(1)}) custom-call(bf16[8,384,256]{2,1,0:T(8,128)(2,1)} %adj_hbm.1, bf16[8,6,384,384]{3,2,1,0:T(8,128)(2,1)} %ops_hbm.1, s32[8,6]{1,0:T(8,128)} %cols_hbm.1, s32[1,2,4]{2,1,0:T(2,128)} %bitcast.5, s32[8,128]{1,0:T(8,128)} %wet_hbm.1, s32[1,256]{1,0:T(1,128)} %bitcast.6, ...), custom_call_target="tpu_custom_call" | custom-call | tf_op jit(solution)/shard_map/adjoint/pallas_call | solution.py:388
  52.3 1.1 %copy.14 = bf16[8,384,256]{2,1,0:T(8,128)(2,1)} copy(bf16[8,384,256]{2,1,0:T(8,128)(2,1)S(1)} %get-tuple-element.4) | data formatting | bytes 3145728
  53.5 1.0 %copy.15 = f32[8,128,256]{2,1,0:T(8,128)} copy(f32[8,128,256]{2,1,0:T(8,128)S(1)} %get-tuple-element.5) | data formatting | bytes 2097152
